TPU v7x, 256 devices: a whole 4x4x8 slice. The times are simulated.
256 devices in a mesh: front: 8 (over x, core), grp: 32 (over y, z).
Axes of the slice: x: 4, y: 4, z: 8, core: 2. Of those that a mesh axis runs over, the one named last changes fastest.
Arguments:
- panel_block: bfloat16 [8, 4608, 1024], P('front', 'grp'), may hold values from -0.1796875 to 0.1796875
- trailing: float32 [8, 4608, 4608], P('front', 'grp')
- inverse: float32 [8, 1024, 1024], P('front')
- weights: float32 [8, 4608], P('front'), may hold values from -0.09375 to 0.09375
- live_size: int32 [8], P('front'), may hold values from 2304 to 4608, as said below
- column_source: int32 [8, 4608], P('front'), may hold values from 0 to 4607, each once within a row
- destination: int32 [8, 4608, 1], P('front', 'grp'), may hold values from 0 to 7; in each aligned block of 144 rows (0 to 143, 144 to 287, ..., all dimensions but the last counted through in order) at most 36 rows name the same one
- row_offset: int32 [8, 4608], P('front', 'grp'), may hold values from 0 to 143
Outputs:
- factor: float32 [8, 4608, 1024], P('front', 'grp')
- checksum: float32 [8, 4608], P('front', 'grp')
- ancestor: float32 [8, 4608, 4608], P('front', 'grp')
Inputs may be any that keep to these rules, and one draw needn't show every extreme that they name: `live_size`: each front's live size is 4608 minus a multiple of 576; one front is full. `destination`: among the 144 rows of one device at most 36 rows name the same ancestor front. `column_source`: each front's row is a permutation.
All inputs are finite; a program needn't handle non-finite values.
Results may differ from a plain program's by a relative error of at most 0.0003.
Values may be sent and summed in bfloat16 or wider, within the bound.
A program may use at most 128 MiB of HBM per device.

v0:
```python
import jax
import jax.numpy as jnp
from jax import lax
from jax.sharding import PartitionSpec as P


def place_columns(rows, source, live_count):
    keep_cols = (source < live_count).astype(jnp.float32)
    return jnp.take(rows, source, axis=1) * keep_cols[None, :]


def on_device(
    panel_block, trailing, inverse, weights, live_size, column_source, destination, row_offset
):
    highest_precision = lax.Precision.HIGHEST
    row_count = trailing.shape[1]
    col_count = trailing.shape[2]
    fronts = lax.axis_size("front")
    capacity = max(2, 2 * row_count // fronts)
    trail_rows = trailing[0]
    inverse_rows = inverse[0]
    live_count = live_size[0]
    panel_f32 = panel_block[0].astype(jnp.float32)
    factor = jnp.dot(panel_f32, inverse_rows.T, precision=highest_precision)
    update = lax.dot_general(
        factor,
        lax.all_gather(factor, "grp", axis=0, tiled=True),
        (((1,), (1,)), ((), ())),
        precision=highest_precision,
        preferred_element_type=jnp.float32,
    )
    schur_rows = trail_rows - update
    positions = jnp.arange(col_count, dtype=jnp.int32)
    colmask = (positions < live_count).astype(jnp.float32)
    masked_weights = weights[0] * colmask
    checksum = jnp.dot(schur_rows, masked_weights, precision=highest_precision)
    global_rows = lax.axis_index("grp") * row_count + jnp.arange(row_count, dtype=jnp.int32)
    live_rows = global_rows < live_count
    dest_front = destination[0, :, 0]
    front_ids = jnp.arange(fronts, dtype=jnp.int32)
    onehot = ((dest_front[:, None] == front_ids[None, :]) & live_rows[:, None]).astype(jnp.int32)
    running = jnp.cumsum(onehot, axis=0)
    slot_index = jnp.sum(onehot * (running - 1), axis=1)
    dest_live = jnp.where(live_rows, dest_front, fronts)
    row_tags = (
        jnp.full((fronts, capacity), -1.0, jnp.float32)
        .at[dest_live, slot_index]
        .set(row_offset[0].astype(jnp.float32), mode="drop")
    )
    permuted = place_columns(schur_rows, column_source[0], live_count)
    bucket = (
        jnp.zeros((fronts, capacity, col_count), jnp.float32)
        .at[dest_live, slot_index]
        .set(permuted, mode="drop")
    )
    received, received_tags = (
        lax.all_to_all(bucket, "front", split_axis=0, concat_axis=0, tiled=True),
        lax.all_to_all(row_tags, "front", split_axis=0, concat_axis=0, tiled=True),
    )
    flat_rows = received.reshape(fronts * capacity, col_count)
    flat_tags = received_tags.reshape(fronts * capacity)
    target_row = jnp.where(flat_tags < 0.0, row_count, flat_tags.astype(jnp.int32))
    ancestor = (
        jnp.zeros((row_count, col_count), jnp.float32).at[target_row].add(flat_rows, mode="drop")
    )
    return (factor[None], checksum[None], ancestor[None])


def solution(mesh):
    placed = (
        P("front", "grp", None),
        P("front", "grp", None),
        P("front", None, None),
        P("front", None),
        P("front"),
        P("front", None),
        P("front", "grp", None),
        P("front", "grp"),
    )
    return jax.shard_map(
        on_device,
        mesh=mesh,
        in_specs=placed,
        out_specs=(P("front", "grp", None), P("front", "grp"), P("front", "grp", None)),
        check_vma=False,
    )
```

profile of v0, /device:TPU:1, one launch (start us, length us, event | category | flops | bytes accessed | tf_op | source)
XLA Modules:
  0.0 366.7 jit_solution(13603879904250098993)
XLA Ops:
  7.2 0.0 copy-start
  7.2 0.0 copy-start.4
  7.2 0.0 copy-start.5
  7.2 0.0 all-gather.2.cloned.1.call-start
  7.3 0.9 copy-done
  8.1 5.4 %fusion = f32[144,1024]{1,0:T(8,128)} fusion(f32[1,1024,1024]{2,1,0:T(8,128)} %param.10, bf16[1,144,1024]{2,1,0:T(8,128)(2,1)S(1)} %copy-done), kind=kOutput, calls=%fused_computation.6 | convolution fusion | flops 1811939328 | bytes 5079040 | tf_op jit(solution)/shard_map/dot_general | solution.py:24
  13.6 0.0 all-gather.2.cloned.1.call-update
  14.3 0.6 reduce-window.6
  14.9 0.2 slice_reduce_fusion
  15.1 0.1 add_bitcast_fusion
  15.3 0.6 broadcast_in_dim.49
  15.9 22.1 %scatter_fusion = f32[8,36]{1,0:T(8,128)} fusion(f32[8,36]{1,0:T(8,128)} %broadcast_in_dim.49, s32[144]{0:T(256)S(1)} %bitcast.39, f32[144]{0:T(256)S(1)} %bitcast.45), kind=kCustom, calls=%fused_computation.1 | custom fusion | bytes 2880 | tf_op jit(solution)/shard_map/scatter | solution.py:48
  37.9 6.4 %all-to-all-start = ((f32[8,1,36]{2,1,0:T(1,128)}), f32[8,1,36]{2,1,0:T(1,128)S(1)}, u32[]{:S(2)}, u32[]{:S(2)}) async-start(f32[8,1,36]{2,1,0:T(1,128)} %bitcast.15), calls=%async_computation | async-start | bytes 8192 | tf_op jit(solution)/shard_map/all_to_all | solution.py:58
  44.4 0.1 fusion.6
  44.5 0.1 fusion.7
  44.6 123.4 %all-gather.2.cloned.1.call-done = f32[4608,1024]{1,0:T(8,128)} async-done(((f32[144,1024]{1,0:T(8,128)}), f32[4608,1024]{1,0:T(8,128)}) %all-gather.2.cloned.1.call-update) | async-done | bytes 18874384 | tf_op jit(solution)/shard_map/all_gather | solution.py:27
  168.0 23.8 %convolution_subtract_fusion = f32[144,4608]{1,0:T(8,128)S(1)} fusion(f32[144,1024]{1,0:T(8,128)} %fusion, f32[4608,1024]{1,0:T(8,128)} %all-gather.2.cloned.1.call-done, f32[1,144,4608]{2,1,0:T(8,128)} %param.9), kind=kOutput, calls=%fused_computation.4 | convolution fusion | flops 8154390528 | bytes 24772608 | tf_op jit(solution)/shard_map/dot_general | solution.py:25
  191.8 3.4 copy.17
  195.2 14.1 %gather_fusion = f32[4608,144]{1,0:T(8,128)} fusion(f32[144,4608]{0,1:T(8,128)} %copy.17, s32[5120]{0:T(1024)S(1)} %pad_clamp_fusion), kind=kCustom, calls=%fused_computation | custom fusion | bytes 5326848 | tf_op jit(solution)/shard_map/jit(_take)/gather | solution.py:9
  209.3 6.4 %multiply_bitcast_fusion = f32[144,4608]{0,1:T(8,128)} fusion(f32[4608,144]{1,0:T(8,128)} %gather_fusion, f32[4608]{0:T(1024)S(1)} %fusion.7, pred[4608]{0:T(1024)(128)(4,1)S(1)} %compare_and_fusion), kind=kLoop, calls=%fused_computation.5 | loop fusion | flops 1327104 | bytes 5331456 | tf_op jit(solution)/shard_map/mul | solution.py:9
  215.7 5.3 %copy.18 = f32[144,4608]{1,0:T(8,128)} copy(f32[144,4608]{0,1:T(8,128)} %multiply_bitcast_fusion) | data formatting | bytes 5308416 | tf_op jit(solution)/shard_map/mul | solution.py:9
  221.0 3.0 broadcast_in_dim.53
  224.0 39.0 %scatter_fusion.1 = f32[8,36,4608]{2,0,1:T(8,128)} fusion(f32[8,36,4608]{2,0,1:T(8,128)} %broadcast_in_dim.53, s32[144]{0:T(256)S(1)} %bitcast.40, f32[144,4608]{1,0:T(8,128)} %copy.18), kind=kCustom, calls=%fused_computation.2 | custom fusion | bytes 7963776 | tf_op jit(solution)/shard_map/scatter | solution.py:54
  263.0 8.1 %copy.19 = f32[8,36,4608]{2,1,0:T(8,128)} copy(f32[8,36,4608]{2,0,1:T(8,128)} %scatter_fusion.1) | data formatting | bytes 10616832 | tf_op jit(solution)/shard_map/scatter | solution.py:54
  271.1 0.0 all-to-all-done
  271.1 5.4 %all-to-all-start.1 = ((f32[8,36,4608]{2,1,0:T(8,128)}), f32[8,36,4608]{2,1,0:T(8,128)}, u32[]{:S(2)}, u32[]{:S(2)}) async-start(f32[8,36,4608]{2,1,0:T(8,128)} %copy.19), calls=%async_computation.1 | async-start | bytes 11796480 | tf_op jit(solution)/shard_map/all_to_all | solution.py:57
  276.7 0.1 select_n.81
  276.8 0.0 copy-start.1
  276.8 2.7 fusion.15
  279.5 64.2 %all-to-all-done.1 = f32[8,36,4608]{2,1,0:T(8,128)} async-done(((f32[8,36,4608]{2,1,0:T(8,128)}), f32[8,36,4608]{2,1,0:T(8,128)}, u32[]{:S(2)}, u32[]{:S(2)}) %all-to-all-start.1) | async-done | bytes 5308448 | tf_op jit(solution)/shard_map/all_to_all | solution.py:57
  343.7 5.6 %reshape.169 = f32[288,4608]{1,0:T(8,128)} reshape(f32[8,36,4608]{2,1,0:T(8,128)} %all-to-all-done.1) | data formatting | bytes 10616832 | tf_op jit(solution)/shard_map/reshape | solution.py:60
  349.3 10.6 %scatter_custom_fusion.2 = f32[144,4608]{1,0:T(8,128)} fusion(s32[288]{0:T(512)S(1)} %fusion.13, f32[288,4608]{1,0:T(8,128)} %reshape.169, f32[]{:T(128)} %constant.13.clone.1), kind=kCustom, calls=%fused_computation.8 | custom fusion | flops 1327104 | bytes 2654720 | tf_op jit(solution)/shard_map/scatter-add | solution.py:64
  (23 shorter events, 0.3 us)
Async XLA Ops:
  7.2 1.0 copy-start
  7.2 7.1 %copy-start.4 = (s32[1,144,1]{1,2,0:T(1,128)S(1)}, s32[1,144,1]{1,2,0:T(1,128)}, u32[]{:S(2)}) copy-start(s32[1,144,1]{1,2,0:T(1,128)} %param.14) | copy-start | bytes 1732
  7.2 7.9 %copy-start.5 = (s32[1,144]{1,0:T(1,128)S(1)}, s32[1,144]{1,0:T(1,128)}, u32[]{:S(2)}) copy-start(s32[1,144]{1,0:T(1,128)} %param.15) | copy-start | bytes 1732
  7.2 37.2 %copy-start.2 = (s32[1,4608]{1,0:T(1,128)S(1)}, s32[1,4608]{1,0:T(1,128)}, u32[]{:S(2)}) copy-start(s32[1,4608]{1,0:T(1,128)} %param.13) | copy-start | bytes 55300
  7.2 160.8 %all-gather.2.cloned.1.call-start = ((), (), s32[]{:S(2)}) async-start(), calls=%async_computation.2 | async-start | bytes 19464192 | tf_op jit(solution)/shard_map/all_gather | solution.py:27
  37.9 233.2 %all-to-all-start = ((f32[8,1,36]{2,1,0:T(1,128)}), f32[8,1,36]{2,1,0:T(1,128)S(1)}, u32[]{:S(2)}, u32[]{:S(2)}) async-start(f32[8,1,36]{2,1,0:T(1,128)} %bitcast.15), calls=%async_computation | async-start | bytes 8192 | tf_op jit(solution)/shard_map/all_to_all | solution.py:58
  271.1 5.4 %copy-start.3 = (f32[1,4608]{1,0:T(1,128)S(1)}, f32[1,4608]{1,0:T(1,128)}, u32[]{:S(2)}) copy-start(f32[1,4608]{1,0:T(1,128)} %param.11) | copy-start | bytes 55300
  271.1 72.6 %all-to-all-start.1 = ((f32[8,36,4608]{2,1,0:T(8,128)}), f32[8,36,4608]{2,1,0:T(8,128)}, u32[]{:S(2)}, u32[]{:S(2)}) async-start(f32[8,36,4608]{2,1,0:T(8,128)} %copy.19), calls=%async_computation.1 | async-start | bytes 11796480 | tf_op jit(solution)/shard_map/all_to_all | solution.py:57
  276.8 83.1 %copy-start.1 = (bf16[1,144,1024]{2,1,0:T(8,128)(2,1)S(1)}, bf16[1,144,1024]{2,1,0:T(8,128)(2,1)}, u32[]{:S(2)}) copy-start(bf16[1,144,1024]{2,1,0:T(8,128)(2,1)} %param.8) | copy-start | bytes 884740
Sparse Core Ops, SparseCore 0:
  13.7 154.2 all-gather.1
where the time goes:
time: 368 us; the launch traced here: 367 us
  waiting for transfers between devices  188 us (51%)
  local copies, waits for them, and re-layouts  102 us (28%)
  matrix products  31.9 us (9%)
  other arithmetic  18 us (5%)
  between operations  14.8 us (4%)
  starting transfers between devices  11.9 us (3%)
    all_gather x1, waiting for transfers between devices, on_device(): lax.all_gather(factor, 'grp', axis=0, tiled=True)  123 us
    all_to_all x1, waiting for transfers between devices, on_device(): lax.all_to_all(bucket, 'front', split_axis=0, concat_axis=0, tiled=True)  64.2 us
    scatter x2, local copies, waits for them, and re-layouts, on_device(): bucket = jnp.zeros((fronts, capacity, col_count), jnp.float32).at[dest_li...  47.1 us
    dot_general x1, matrix products, on_device(): lax.dot_general(factor, lax.all_gather(factor, 'grp', axis=0, tiled=True)...  23.8 us
    scatter x1, local copies, waits for them, and re-layouts, on_device(): row_tags = jnp.full((fronts, capacity), -1.0, jnp.float32).at[dest_live,...  22.1 us
    gather x1, local copies, waits for them, and re-layouts, place_columns(): return jnp.take(rows, source, axis=1) * keep_cols[None, :]  14.1 us
    scatter-add x1, other arithmetic, on_device(): jnp.zeros((row_count, col_count), jnp.float32).at[target_row]  10.6 us
  transfers between devices with their start and end apart: 3, of which 2 were waited for; matrix products, arithmetic and copies ran while one was open for 35% of the time, Pallas kernels for 0%

commit v1 on v0

--- a/solution.py
+++ b/solution.py
@@ -24,7 +24,9 @@
     factor = jnp.dot(panel_f32, inverse_rows.T, precision=highest_precision)
     update = lax.dot_general(
         factor,
-        lax.all_gather(factor, "grp", axis=0, tiled=True),
+        jnp.concatenate(
+            lax.all_to_all(jnp.stack([factor] * lax.axis_size("grp")), "grp", 0, 0), axis=0
+        ),
         (((1,), (1,)), ((), ())),
         precision=highest_precision,
         preferred_element_type=jnp.float32,

time: 368 us -> 682 us (1.85)
  the two profiles are of different devices: /device:TPU:1 before, /device:TPU:184 now
where the time goes in v1:
time: 682 us; the launch traced here: 680 us
  waiting for transfers between devices  503 us (74%)
  local copies, waits for them, and re-layouts  108 us (16%)
  matrix products  31.1 us (5%)
  starting transfers between devices  18.7 us (3%)
  other arithmetic  18 us (3%)
    all_to_all x1, waiting for transfers between devices, on_device(): lax.all_to_all(jnp.stack([factor] * lax.axis_size('grp')), 'grp', 0, 0)  438 us
    all_to_all x1, waiting for transfers between devices, on_device(): lax.all_to_all(bucket, 'front', split_axis=0, concat_axis=0, tiled=True)  65.1 us
    scatter x2, local copies, waits for them, and re-layouts, on_device(): bucket = jnp.zeros((fronts, capacity, col_count), jnp.float32).at[dest_li...  49.1 us
    dot_general x1, matrix products, on_device(): lax.dot_general(factor, jnp.concatenate(lax.all_to_all(jnp.stack([factor]...  23.7 us
    scatter x1, local copies, waits for them, and re-layouts, on_device(): row_tags = jnp.full((fronts, capacity), -1.0, jnp.float32).at[dest_live,...  17 us
    gather x1, local copies, waits for them, and re-layouts, place_columns(): return jnp.take(rows, source, axis=1) * keep_cols[None, :]  14.1 us
  transfers between devices with their start and end apart: 3, of which 2 were waited for; matrix products, arithmetic and copies ran while one was open for 19% of the time, Pallas kernels for 0%

profile of v1, /device:TPU:184, one launch (start us, length us, event | category | flops | bytes accessed | tf_op | source)
XLA Modules:
  0.0 680.1 jit_solution(12196984543663282156)
XLA Ops:
  0.6 0.0 copy-start
  0.6 1.0 copy-done
  1.6 4.6 fusion
  6.2 0.0 copy-start.2
  6.2 8.9 %stack.2 = f32[32,144,1024]{2,1,0:T(8,128)} broadcast(f32[144,1024]{1,0:T(8,128)S(1)} %fusion), dimensions={1,2} | broadcast | bytes 19464192 | tf_op jit(solution)/shard_map/stack | solution.py:28
  15.1 9.5 %all-to-all-start = ((f32[32,144,1024]{2,1,0:T(8,128)}), f32[32,144,1024]{2,1,0:T(8,128)}, u32[]{:S(2)}, u32[]{:S(2)}) async-start(f32[32,144,1024]{2,1,0:T(8,128)} %stack.2), calls=%async_computation | async-start | bytes 37748736 | tf_op jit(solution)/shard_map/all_to_all | solution.py:28
  25.3 0.0 copy-done.5
  25.3 0.6 reduce-window.6
  25.9 0.2 slice_reduce_fusion
  26.2 0.1 add_bitcast_fusion
  26.3 0.6 broadcast_in_dim.49
  26.9 17.0 %scatter_fusion = f32[8,36]{1,0:T(8,128)} fusion(f32[8,36]{1,0:T(8,128)} %broadcast_in_dim.49, s32[144]{0:T(256)S(1)} %bitcast.40, f32[144]{0:T(256)S(1)} %bitcast.46), kind=kCustom, calls=%fused_computation.1 | custom fusion | bytes 2880 | tf_op jit(solution)/shard_map/scatter | solution.py:50
  43.9 0.1 fusion.6
  44.0 0.1 fusion.7
  44.1 437.6 %all-to-all-done = f32[32,144,1024]{2,1,0:T(8,128)} async-done(((f32[32,144,1024]{2,1,0:T(8,128)}), f32[32,144,1024]{2,1,0:T(8,128)}, u32[]{:S(2)}, u32[]{:S(2)}) %all-to-all-start) | async-done | bytes 18874400 | tf_op jit(solution)/shard_map/all_to_all | solution.py:28
  481.7 4.3 all-to-all-start.1
  486.0 23.7 %convolution_subtract_fusion = f32[144,4608]{1,0:T(8,128)S(1)} fusion(f32[144,1024]{1,0:T(8,128)S(1)} %fusion, f32[4608,1024]{1,0:T(8,128)} %bitcast.4, f32[1,144,4608]{2,1,0:T(8,128)} %param.9), kind=kOutput, calls=%fused_computation.4 | convolution fusion | flops 8154390528 | bytes 24772608 | tf_op jit(solution)/shard_map/dot_general | solution.py:25
  509.7 3.4 copy.17
  513.1 14.1 %gather_fusion = f32[4608,144]{1,0:T(8,128)} fusion(f32[144,4608]{0,1:T(8,128)} %copy.17, s32[5120]{0:T(1024)S(1)} %pad_clamp_fusion), kind=kCustom, calls=%fused_computation | custom fusion | bytes 5326848 | tf_op jit(solution)/shard_map/jit(_take)/gather | solution.py:9
  527.2 6.4 multiply_bitcast_fusion
  533.7 5.3 copy.18
  538.9 3.0 broadcast_in_dim.53
  541.9 41.0 %scatter_fusion.1 = f32[8,36,4608]{2,0,1:T(8,128)} fusion(f32[8,36,4608]{2,0,1:T(8,128)} %broadcast_in_dim.53, s32[144]{0:T(256)S(1)} %bitcast.41, f32[144,4608]{1,0:T(8,128)} %copy.18), kind=kCustom, calls=%fused_computation.2 | custom fusion | bytes 7963776 | tf_op jit(solution)/shard_map/scatter | solution.py:56
  582.9 8.1 %copy.19 = f32[8,36,4608]{2,1,0:T(8,128)} copy(f32[8,36,4608]{2,0,1:T(8,128)} %scatter_fusion.1) | data formatting | bytes 10616832 | tf_op jit(solution)/shard_map/scatter | solution.py:56
  591.0 0.0 all-to-all-done.1
  591.0 4.9 all-to-all-start.2
  596.1 0.1 select_n.81
  596.2 0.0 copy-start.1
  596.2 2.7 fusion.15
  598.9 65.1 %all-to-all-done.2 = f32[8,36,4608]{2,1,0:T(8,128)} async-done(((f32[8,36,4608]{2,1,0:T(8,128)}), f32[8,36,4608]{2,1,0:T(8,128)}, u32[]{:S(2)}, u32[]{:S(2)}) %all-to-all-start.2) | async-done | bytes 5308448 | tf_op jit(solution)/shard_map/all_to_all | solution.py:59
  664.0 5.6 reshape.175
  669.6 10.6 %scatter_custom_fusion.2 = f32[144,4608]{1,0:T(8,128)} fusion(s32[288]{0:T(512)S(1)} %fusion.13, f32[288,4608]{1,0:T(8,128)} %reshape.175, f32[]{:T(128)} %constant.13.clone.1), kind=kCustom, calls=%fused_computation.8 | custom fusion | flops 1327104 | bytes 2654720 | tf_op jit(solution)/shard_map/scatter-add | solution.py:66
  (25 shorter events, 0.3 us)
Async XLA Ops:
  0.6 1.0 copy-start
  6.2 479.8 %copy-start.2 = (f32[144,1024]{1,0:T(8,128)}, f32[144,1024]{1,0:T(8,128)S(1)}, u32[]{:S(2)}) copy-start(f32[144,1024]{1,0:T(8,128)S(1)} %fusion) | copy-start | bytes 1769476
  15.1 10.1 %copy-start.5 = (s32[1,144,1]{1,2,0:T(1,128)S(1)}, s32[1,144,1]{1,2,0:T(1,128)}, u32[]{:S(2)}) copy-start(s32[1,144,1]{1,2,0:T(1,128)} %param.14) | copy-start | bytes 1732
  15.1 11.0 %copy-start.6 = (s32[1,144]{1,0:T(1,128)S(1)}, s32[1,144]{1,0:T(1,128)}, u32[]{:S(2)}) copy-start(s32[1,144]{1,0:T(1,128)} %param.15) | copy-start | bytes 1732
  15.1 11.0 %copy-start.3 = (s32[1,4608]{1,0:T(1,128)S(1)}, s32[1,4608]{1,0:T(1,128)}, u32[]{:S(2)}) copy-start(s32[1,4608]{1,0:T(1,128)} %param.13) | copy-start | bytes 55300
  15.1 466.6 %all-to-all-start = ((f32[32,144,1024]{2,1,0:T(8,128)}), f32[32,144,1024]{2,1,0:T(8,128)}, u32[]{:S(2)}, u32[]{:S(2)}) async-start(f32[32,144,1024]{2,1,0:T(8,128)} %stack.2), calls=%async_computation | async-start | bytes 37748736 | tf_op jit(solution)/shard_map/all_to_all | solution.py:28
  481.7 109.3 %all-to-all-start.1 = ((f32[8,1,36]{2,1,0:T(1,128)}), f32[8,1,36]{2,1,0:T(1,128)S(1)}, u32[]{:S(2)}, u32[]{:S(2)}) async-start(f32[8,1,36]{2,1,0:T(1,128)} %bitcast.16), calls=%async_computation.1 | async-start | bytes 8192 | tf_op jit(solution)/shard_map/all_to_all | solution.py:60
  591.0 4.9 copy-start.4
  591.0 73.0 %all-to-all-start.2 = ((f32[8,36,4608]{2,1,0:T(8,128)}), f32[8,36,4608]{2,1,0:T(8,128)}, u32[]{:S(2)}, u32[]{:S(2)}) async-start(f32[8,36,4608]{2,1,0:T(8,128)} %copy.19), calls=%async_computation.2 | async-start | bytes 11796480 | tf_op jit(solution)/shard_map/all_to_all | solution.py:59
  596.2 83.9 %copy-start.1 = (bf16[1,144,1024]{2,1,0:T(8,128)(2,1)S(1)}, bf16[1,144,1024]{2,1,0:T(8,128)(2,1)}, u32[]{:S(2)}) copy-start(bf16[1,144,1024]{2,1,0:T(8,128)(2,1)} %param.8) | copy-start | bytes 884740
